TPU v7x, 32 devices: a whole 2x2x4 slice. The times are simulated.
32 devices in a mesh: face: 2 (over x), patch: 16 (over z, y, core).
Axes of the slice: x: 2, y: 2, z: 4, core: 2. Of those that a mesh axis runs over, the one named last changes fastest.
Arguments:
- features: bfloat16 [32, 2, 65536], P(None, 'face', 'patch'), may hold values from -6 to 6
- film_first: float32 [2, 32], replicated, may hold values from -3 to 3
- weight_first: bfloat16 [32, 288], replicated, may hold values from -0.375 to 0.375
- film_second: float32 [2, 32], replicated, may hold values from -3 to 3
- weight_second: bfloat16 [64, 288], replicated, may hold values from -0.375 to 0.375
- film_third: float32 [2, 64], replicated, may hold values from -3 to 3
- weight_third: bfloat16 [128, 576], replicated, may hold values from -0.25 to 0.25
- film_fourth: float32 [2, 128], replicated, may hold values from -3 to 3
- weight_fourth: bfloat16 [128, 1152], replicated, may hold values from -0.1875 to 0.1875
- film_fifth: float32 [2, 192], replicated, may hold values from -3 to 3
- weight_fifth: bfloat16 [64, 1728], replicated, may hold values from -0.15625 to 0.15625
- film_sixth: float32 [2, 96], replicated, may hold values from -3 to 3
- weight_sixth: bfloat16 [32, 864], replicated, may hold values from -0.21875 to 0.21875
- link_patch: int32 [2, 16, 8], replicated, may hold values from 0 to 15, as said below
- link_shift: int32 [2, 16, 8], replicated, may hold values from -1 to 1, as said below
- link_turn: int32 [2, 16, 8], replicated, may hold values from 0 to 3, as said below
Outputs:
- denoised: bfloat16 [32, 2, 65536], P(None, 'face', 'patch')
Inputs may be any that keep to these rules, and one draw needn't show every extreme that they name: `link_patch`: patch p of a face sits at row p // 4 and column p % 4 of a 4 x 4 grid of patches. For a direction that stays inside that grid the entry is the grid neighbour. For a direction that leaves it the entry is a patch on the outer row or column of the neighbouring face's grid such that every cell that padded reads from it lies on that face's outer border. `link_shift`: 0 for a direction that stays inside the face's grid of patches, -1 or +1 for one that leaves it. `link_turn`: 0 for a direction that stays inside the face's grid of patches.
All inputs are finite; a program needn't handle non-finite values.
Results may differ from a plain program's by a relative error of at most 0.009.
Values may be sent and summed in bfloat16 or wider, within the bound.
A program may use at most 128 MiB of HBM per device.

v0:
```python
import math

import jax
import jax.numpy as jnp
from jax import lax
from jax.sharding import PartitionSpec as P

EPSILON = 1e-05
FLOOR_SQUARE = 0.5


def shifted(array, axis, by):
    devices = lax.axis_size(axis)
    return lax.ppermute(array, axis, [(i, (i + by) % devices) for i in range(devices)])


def activate(values, modulation):
    channels = values.shape[-2]
    mean_square = jnp.mean(values * values, axis=-2, keepdims=True)
    if channels >= 64:
        inverse = lax.rsqrt(mean_square + EPSILON)
    else:
        inverse = lax.rsqrt(jnp.maximum(mean_square, FLOOR_SQUARE))
    shaped = values * inverse * (1.0 + modulation[0][:, None]) + modulation[1][:, None]
    return jax.nn.silu(shaped).astype(jnp.bfloat16)


def frame_of(grids):
    return jnp.stack(
        [grids[..., 0, :], grids[..., -1, :], grids[..., :, 0], grids[..., :, -1]], axis=-3
    )


def turn_once(frames):
    return jnp.stack(
        [
            frames[..., 3, :, :],
            frames[..., 2, :, :],
            frames[..., 0, :, ::-1],
            frames[..., 1, :, ::-1],
        ],
        axis=-3,
    )


def turned(frames, quarters):
    result = frames
    current = frames
    for count in range(1, 4):
        current = turn_once(current)
        result = jnp.where((quarters == count)[:, None, None, None], current, result)
    return result


def cycle_of(frames):
    edges = jnp.stack([frames[0, 1], frames[1, 0], frames[2, 3], frames[3, 2]])
    corners = jnp.stack(
        [frames[4, 1, :, -1], frames[5, 1, :, 0], frames[6, 0, :, -1], frames[7, 0, :, 0]]
    )
    return (edges, corners)


def assemble(grid, edges, corners):
    middle = jnp.concatenate([edges[2][:, :, None], grid, edges[3][:, :, None]], axis=2)
    upper = jnp.concatenate([corners[0][:, None], edges[0], corners[1][:, None]], axis=1)
    lowest = jnp.concatenate([corners[2][:, None], edges[1], corners[3][:, None]], axis=1)
    return jnp.concatenate([upper[:, None, :], middle, lowest[:, None, :]], axis=1)


def stencil(padded, weight):
    channels = padded.shape[0]
    length = padded.shape[1] - 2
    columns = [
        padded[:, row_start : row_start + length, col_start : col_start + length].reshape(
            channels, length * length
        )
        for row_start in range(3)
        for col_start in range(3)
    ]
    return jnp.dot(weight, jnp.concatenate(columns, axis=0), preferred_element_type=jnp.float32)


def pieces_for(face_frames, tables, target_face, patch_id):
    link_patch, link_shift, link_turn = tables
    wanted = face_frames[link_patch[target_face, patch_id]]
    return cycle_of(turned(wanted, link_turn[target_face, patch_id]))


def select_cycle(near_shift, own_edges, own_corners, from_below, from_above):
    edge_shift = near_shift[:4][:, None, None]
    corner_shift = near_shift[4:][:, None]
    edges = jnp.where(
        edge_shift == 0, own_edges, jnp.where(edge_shift < 0, from_below[0], from_above[0])
    )
    corners = jnp.where(
        corner_shift == 0, own_corners, jnp.where(corner_shift < 0, from_below[1], from_above[1])
    )
    return (edges, corners)


def level_conv(active, weight, tables, face_id, patch_id, face_count):
    link_patch, link_shift, link_turn = tables
    channels, cells = active.shape
    length = math.isqrt(cells)
    grid = active.reshape(channels, length, length)
    near_patch = link_patch[face_id, patch_id]
    near_shift = link_shift[face_id, patch_id]
    near_turn = link_turn[face_id, patch_id]
    above_face = jnp.mod(face_id + 1, face_count)
    below_face = jnp.mod(face_id - 1, face_count)
    own_frame = frame_of(grid)
    face_frames = lax.all_gather(own_frame[None], "patch", axis=0, tiled=True)
    own_edges, own_corners = cycle_of(turned(face_frames[near_patch], near_turn))
    for_above = pieces_for(face_frames, tables, above_face, patch_id)
    for_below = pieces_for(face_frames, tables, below_face, patch_id)
    from_below = shifted((for_above[0], for_above[1]), "face", 1)
    from_above = shifted((for_below[0], for_below[1]), "face", -1)
    edges, corners = select_cycle(near_shift, own_edges, own_corners, from_below, from_above)
    return stencil(assemble(grid, edges, corners), weight)


def coarsen(field):
    channels, cells = field.shape
    length = math.isqrt(cells)
    half_side = length // 2
    blocks = field.reshape(channels, half_side, 2, half_side, 2)
    return jnp.mean(blocks, axis=(2, 4)).reshape(channels, half_side * half_side)


def refine(field):
    channels, cells = field.shape
    length = math.isqrt(cells)
    grid = field.reshape(channels, length, length)
    grid = jnp.repeat(jnp.repeat(grid, 2, axis=1), 2, axis=2)
    return grid.reshape(channels, 4 * length * length)


def body(
    features,
    film_first,
    weight_first,
    film_second,
    weight_second,
    film_third,
    weight_third,
    film_fourth,
    weight_fourth,
    film_fifth,
    weight_fifth,
    film_sixth,
    weight_sixth,
    link_patch,
    link_shift,
    link_turn,
):
    face_id = lax.axis_index("face")
    patch_id = lax.axis_index("patch")
    face_count = lax.axis_size("face")
    tables = (link_patch, link_shift, link_turn)

    def apply_conv(active, weight):
        return level_conv(active, weight, tables, face_id, patch_id, face_count)

    fine = features[:, 0, :].astype(jnp.float32)
    first = fine + apply_conv(activate(fine, film_first), weight_first)
    skip_fine = first.astype(jnp.bfloat16)
    second = apply_conv(activate(coarsen(first), film_second), weight_second)
    skip_middle = second.astype(jnp.bfloat16)
    third = apply_conv(activate(coarsen(second), film_third), weight_third)
    fourth = third + apply_conv(activate(third, film_fourth), weight_fourth)
    joined_middle = jnp.concatenate([refine(fourth), skip_middle.astype(jnp.float32)], axis=0)
    fifth = apply_conv(activate(joined_middle, film_fifth), weight_fifth)
    joined_fine = jnp.concatenate([refine(fifth), skip_fine.astype(jnp.float32)], axis=0)
    result = skip_fine.astype(jnp.float32) + apply_conv(
        activate(joined_fine, film_sixth), weight_sixth
    )
    return result.astype(jnp.bfloat16)[:, None, :]


def solution(mesh):
    in_specs = (
        P(None, "face", "patch"),
        P(),
        P(),
        P(),
        P(),
        P(),
        P(),
        P(),
        P(),
        P(),
        P(),
        P(),
        P(),
        P(),
        P(),
        P(),
    )
    out_specs = P(None, "face", "patch")
    return jax.shard_map(body, mesh=mesh, in_specs=in_specs, out_specs=out_specs, check_vma=False)
```

profile of v0, /device:TPU:0, one launch (start us, length us, event | category | flops | bytes accessed | tf_op | source)
XLA Modules:
  0.0 423.4 jit_solution(7849841603008519442)
XLA Ops:
  7.0 24.8 %all-gather = bf16[64,32,64]{2,1,0:T(8,128)(2,1)S(1)} all-gather(bf16[4,32,64]{2,1,0:T(8,128)(2,1)S(1)} %pad_maximum_fusion.26), channel_id=2, replica_groups=mesh['face'=2,'patch'=16] {'patch'}, dimensions={0}, use_global_device_ids=true | all-gather | bytes 278528 | tf_op jit(solution)/shard_map/all_gather | solution.py:112
  65.5 3.3 reduce_sum.77
  70.8 18.7 %all-gather.1 = bf16[64,32,32]{2,1,0:T(8,128)(2,1)S(1)} all-gather(bf16[4,32,32]{2,1,0:T(8,128)(2,1)S(1)} %pad_maximum_fusion.29), channel_id=3, replica_groups=mesh['face'=2,'patch'=16] {'patch'}, dimensions={0}, use_global_device_ids=true | all-gather | bytes 139264 | tf_op jit(solution)/shard_map/all_gather | solution.py:112
  114.8 3.0 copy.526
  141.2 20.1 %all-gather.2 = bf16[64,64,16]{1,2,0:T(8,128)(2,1)S(1)} all-gather(bf16[4,64,16]{1,2,0:T(8,128)(2,1)S(1)} %pad_maximum_fusion.32), channel_id=4, replica_groups=mesh['face'=2,'patch'=16] {'patch'}, dimensions={0}, use_global_device_ids=true | all-gather | bytes 139264 | tf_op jit(solution)/shard_map/all_gather | solution.py:112
  183.5 18.0 %all-gather.3 = bf16[64,128,16]{1,2,0:T(8,128)(2,1)S(1)} all-gather(bf16[4,128,16]{1,2,0:T(8,128)(2,1)S(1)} %pad_maximum_fusion.35), channel_id=5, replica_groups=mesh['face'=2,'patch'=16] {'patch'}, dimensions={0}, use_global_device_ids=true | all-gather | bytes 278528 | tf_op jit(solution)/shard_map/all_gather | solution.py:112
  218.9 22.1 %all-gather.4 = bf16[64,192,32]{1,2,0:T(8,128)(2,1)S(1)} all-gather(bf16[4,192,32]{1,2,0:T(8,128)(2,1)S(1)} %pad_maximum_fusion.21), channel_id=6, replica_groups=mesh['face'=2,'patch'=16] {'patch'}, dimensions={0}, use_global_device_ids=true | all-gather | bytes 835584 | tf_op jit(solution)/shard_map/all_gather | solution.py:112
  287.8 7.0 %concatenate.237 = bf16[1728,1024]{0,1:T(8,128)(2,1)} concatenate(bf16[192,1024]{0,1:T(8,128)(2,1)} %bitcast.639, bf16[192,1024]{0,1:T(8,128)(2,1)} %bitcast.638, bf16[192,1024]{0,1:T(8,128)(2,1)} %bitcast.637, bf16[192,1024]{0,1:T(8,128)(2,1)} %bitcast.633, bf16[192,1024]{0,1:T(8,128)(2,1)S(1)} %copy-done.23, bf16[192,1024]{0,1:T(8,128)(2,1)S(1)} %bitcast.632, ...), dimensions={0} | concatenate | bytes 7077888 | tf_op jit(solution)/shard_map/concatenate | solution.py:80
  294.8 3.3 convolution_bitcast_fusion.3
  305.2 3.6 multiply_convert_fusion.1
  312.9 2.5 copy.567
  316.9 20.6 %all-gather.5 = bf16[64,96,64]{1,2,0:T(8,128)(2,1)S(1)} all-gather(bf16[4,96,64]{1,2,0:T(8,128)(2,1)S(1)} %copy.534), channel_id=7, replica_groups=mesh['face'=2,'patch'=16] {'patch'}, dimensions={0}, use_global_device_ids=true | all-gather | bytes 835584 | tf_op jit(solution)/shard_map/all_gather | solution.py:112
  371.9 3.4 copy.544
  375.2 2.4 copy.542
  377.6 3.5 pad_maximum_fusion.1
  381.1 2.9 fusion.22
  384.0 3.4 copy.548
  387.4 3.4 copy.547
  393.1 2.4 fusion.23
  395.5 3.5 copy.540
  399.1 2.3 copy.539
  401.4 2.4 copy.538
  403.8 13.2 %concatenate.249 = bf16[864,4096]{0,1:T(8,128)(2,1)} concatenate(bf16[96,4096]{0,1:T(8,128)(2,1)} %bitcast.623, bf16[96,4096]{0,1:T(8,128)(2,1)} %bitcast.622, bf16[96,4096]{0,1:T(8,128)(2,1)} %bitcast.621, bf16[96,4096]{0,1:T(8,128)(2,1)} %bitcast.617, bf16[96,4096]{0,1:T(8,128)(2,1)} %multiply_convert_fusion.1, bf16[96,4096]{0,1:T(8,128)(2,1)S(1)} %bitcast.616, ...), dimensions={0} | concatenate | bytes 14155776 | tf_op jit(solution)/shard_map/concatenate | solution.py:80
  417.0 6.1 %fusion.3 = bf16[32,1,4096]{2,0,1:T(8,128)(2,1)} fusion(bf16[864,4096]{0,1:T(8,128)(2,1)} %concatenate.249, bf16[32,864]{1,0:T(8,128)(2,1)S(1)} %copy-done.33, f32[32,4096]{1,0:T(8,128)S(1)} %copy-done.14), kind=kOutput, calls=%fused_computation.23 | convolution fusion | flops 227016704 | bytes 7919616 | tf_op jit(solution)/shard_map/dot_general | solution.py:80
  (684 shorter events, 224.8 us)
Async XLA Ops:
  33.3 10.7 %collective-permute-start = (bf16[4,32]{1,0:T(4,128)(2,1)S(1)}, bf16[4,32]{1,0:T(4,128)(2,1)S(1)}, u32[]{:S(2)}, u32[]{:S(2)}) collective-permute-start(bf16[4,32]{1,0:T(4,128)(2,1)S(1)} %pad_maximum_fusion.40), channel_id=1, source_target_pairs={{0,16},{16,0},{1,17},{17,1},{2,18},{18,2},{3,19},{19,3},{4,20},{20... | collective-permute-start | bytes 776 | tf_op jit(solution)/shard_map/ppermute | solution.py:14
  34.9 9.7 %collective-permute-start.2 = (bf16[4,32,64]{2,1,0:T(8,128)(2,1)S(1)}, bf16[4,32,64]{2,1,0:T(8,128)(2,1)S(1)}, u32[]{:S(2)}, u32[]{:S(2)}) collective-permute-start(bf16[4,32,64]{2,1,0:T(8,128)(2,1)S(1)} %pad_maximum_fusion.27), channel_id=1, source_target_pairs={{0,16},{16,0},{1,17},{17,1},{2,18},{18,2},{3,19},{19,3},{4,20},{20... | collective-permute-start | bytes 49160 | tf_op jit(solution)/shard_map/ppermute | solution.py:14
  37.1 7.0 %collective-permute-start.1 = (bf16[4,32]{1,0:T(4,128)(2,1)S(1)}, bf16[4,32]{1,0:T(4,128)(2,1)S(1)}, u32[]{:S(2)}, u32[]{:S(2)}) collective-permute-start(bf16[4,32]{1,0:T(4,128)(2,1)S(1)} %pad_maximum_fusion.41), channel_id=1, source_target_pairs={{0,16},{16,0},{1,17},{17,1},{2,18},{18,2},{3,19},{19,3},{4,20},{20... | collective-permute-start | bytes 776 | tf_op jit(solution)/shard_map/ppermute | solution.py:14
  38.7 5.9 %collective-permute-start.3 = (bf16[4,32,64]{2,1,0:T(8,128)(2,1)S(1)}, bf16[4,32,64]{2,1,0:T(8,128)(2,1)S(1)}, u32[]{:S(2)}, u32[]{:S(2)}) collective-permute-start(bf16[4,32,64]{2,1,0:T(8,128)(2,1)S(1)} %pad_maximum_fusion.28), channel_id=1, source_target_pairs={{0,16},{16,0},{1,17},{17,1},{2,18},{18,2},{3,19},{19,3},{4,20},{20... | collective-permute-start | bytes 49160 | tf_op jit(solution)/shard_map/ppermute | solution.py:14
  119.3 4.4 %collective-permute-start.4 = (bf16[4,32]{1,0:T(4,128)(2,1)S(1)}, bf16[4,32]{1,0:T(4,128)(2,1)S(1)}, u32[]{:S(2)}, u32[]{:S(2)}) collective-permute-start(bf16[4,32]{1,0:T(4,128)(2,1)S(1)} %pad_maximum_fusion.42), channel_id=1, source_target_pairs={{0,16},{16,0},{1,17},{17,1},{2,18},{18,2},{3,19},{19,3},{4,20},{20... | collective-permute-start | bytes 776 | tf_op jit(solution)/shard_map/ppermute | solution.py:14
  120.9 5.4 %collective-permute-start.6 = (bf16[4,32,32]{2,1,0:T(8,128)(2,1)S(1)}, bf16[4,32,32]{2,1,0:T(8,128)(2,1)S(1)}, u32[]{:S(2)}, u32[]{:S(2)}) collective-permute-start(bf16[4,32,32]{2,1,0:T(8,128)(2,1)S(1)} %pad_maximum_fusion.30), channel_id=1, source_target_pairs={{0,16},{16,0},{1,17},{17,1},{2,18},{18,2},{3,19},{19,3},{4,20},{20... | collective-permute-start | bytes 24584 | tf_op jit(solution)/shard_map/ppermute | solution.py:14
  121.5 3.6 collective-permute-start.5
  123.0 4.0 collective-permute-start.7
  170.3 4.4 %collective-permute-start.8 = (bf16[4,64]{1,0:T(4,128)(2,1)S(1)}, bf16[4,64]{1,0:T(4,128)(2,1)S(1)}, u32[]{:S(2)}, u32[]{:S(2)}) collective-permute-start(bf16[4,64]{1,0:T(4,128)(2,1)S(1)} %pad_maximum_fusion.44), channel_id=1, source_target_pairs={{0,16},{16,0},{1,17},{17,1},{2,18},{18,2},{3,19},{19,3},{4,20},{20... | collective-permute-start | bytes 1544 | tf_op jit(solution)/shard_map/ppermute | solution.py:14
  171.1 5.7 %collective-permute-start.10 = (bf16[4,64,16]{1,2,0:T(8,128)(2,1)S(1)}, bf16[4,64,16]{1,2,0:T(8,128)(2,1)S(1)}, u32[]{:S(2)}, u32[]{:S(2)}) collective-permute-start(bf16[4,64,16]{1,2,0:T(8,128)(2,1)S(1)} %pad_maximum_fusion.33), channel_id=1, source_target_pairs={{0,16},{16,0},{1,17},{17,1},{2,18},{18,2},{3,19},{19,3},{4,20},{20... | collective-permute-start | bytes 24584 | tf_op jit(solution)/shard_map/ppermute | solution.py:14
  172.5 3.6 collective-permute-start.9
  173.3 3.8 collective-permute-start.11
  205.7 4.2 collective-permute-start.12
  207.0 5.2 %collective-permute-start.14 = (bf16[4,128,16]{1,2,0:T(8,128)(2,1)S(1)}, bf16[4,128,16]{1,2,0:T(8,128)(2,1)S(1)}, u32[]{:S(2)}, u32[]{:S(2)}) collective-permute-start(bf16[4,128,16]{1,2,0:T(8,128)(2,1)S(1)} %pad_maximum_fusion.36), channel_id=1, source_target_pairs={{0,16},{16,0},{1,17},{17,1},{2,18},{18,2},{3,19},{19,3},{4,20},{20... | collective-permute-start | bytes 49160 | tf_op jit(solution)/shard_map/ppermute | solution.py:14
  207.8 3.6 collective-permute-start.13
  209.1 3.7 collective-permute-start.15
  269.6 4.4 %collective-permute-start.16 = (bf16[4,192]{1,0:T(4,128)(2,1)S(1)}, bf16[4,192]{1,0:T(4,128)(2,1)S(1)}, u32[]{:S(2)}, u32[]{:S(2)}) collective-permute-start(bf16[4,192]{1,0:T(4,128)(2,1)S(1)} %pad_maximum_fusion.38), channel_id=1, source_target_pairs={{0,16},{16,0},{1,17},{17,1},{2,18},{18,2},{3,19},{19,3},{4,20},{20... | collective-permute-start | bytes 4616 | tf_op jit(solution)/shard_map/ppermute | solution.py:14
  270.5 5.7 %collective-permute-start.18 = (bf16[4,192,32]{1,2,0:T(8,128)(2,1)S(1)}, bf16[4,192,32]{1,2,0:T(8,128)(2,1)S(1)}, u32[]{:S(2)}, u32[]{:S(2)}) collective-permute-start(bf16[4,192,32]{1,2,0:T(8,128)(2,1)S(1)} %pad_maximum_fusion.22), channel_id=1, source_target_pairs={{0,16},{16,0},{1,17},{17,1},{2,18},{18,2},{3,19},{19,3},{4,20},{20... | collective-permute-start | bytes 147464 | tf_op jit(solution)/shard_map/ppermute | solution.py:14
  271.8 3.7 collective-permute-start.17
  272.7 4.3 %collective-permute-start.19 = (bf16[4,192,32]{1,2,0:T(8,128)(2,1)S(1)}, bf16[4,192,32]{1,2,0:T(8,128)(2,1)S(1)}, u32[]{:S(2)}, u32[]{:S(2)}) collective-permute-start(bf16[4,192,32]{1,2,0:T(8,128)(2,1)S(1)} %pad_maximum_fusion.23), channel_id=1, source_target_pairs={{0,16},{16,0},{1,17},{17,1},{2,18},{18,2},{3,19},{19,3},{4,20},{20... | collective-permute-start | bytes 147464 | tf_op jit(solution)/shard_map/ppermute | solution.py:14
  357.8 4.4 %collective-permute-start.20 = (bf16[4,96]{1,0:T(4,128)(2,1)S(1)}, bf16[4,96]{1,0:T(4,128)(2,1)S(1)}, u32[]{:S(2)}, u32[]{:S(2)}) collective-permute-start(bf16[4,96]{1,0:T(4,128)(2,1)S(1)} %pad_maximum_fusion.48), channel_id=1, source_target_pairs={{0,16},{16,0},{1,17},{17,1},{2,18},{18,2},{3,19},{19,3},{4,20},{20... | collective-permute-start | bytes 2312 | tf_op jit(solution)/shard_map/ppermute | solution.py:14
  359.1 5.3 %collective-permute-start.22 = (bf16[4,96,64]{1,2,0:T(8,128)(2,1)S(1)}, bf16[4,96,64]{1,2,0:T(8,128)(2,1)S(1)}, u32[]{:S(2)}, u32[]{:S(2)}) collective-permute-start(bf16[4,96,64]{1,2,0:T(8,128)(2,1)S(1)} %pad_maximum_fusion.24), channel_id=1, source_target_pairs={{0,16},{16,0},{1,17},{17,1},{2,18},{18,2},{3,19},{19,3},{4,20},{20... | collective-permute-start | bytes 147464 | tf_op jit(solution)/shard_map/ppermute | solution.py:14
  360.0 3.6 collective-permute-start.21
  361.3 4.3 %collective-permute-start.23 = (bf16[4,96,64]{1,2,0:T(8,128)(2,1)S(1)}, bf16[4,96,64]{1,2,0:T(8,128)(2,1)S(1)}, u32[]{:S(2)}, u32[]{:S(2)}) collective-permute-start(bf16[4,96,64]{1,2,0:T(8,128)(2,1)S(1)} %pad_maximum_fusion.25), channel_id=1, source_target_pairs={{0,16},{16,0},{1,17},{17,1},{2,18},{18,2},{3,19},{19,3},{4,20},{20... | collective-permute-start | bytes 147464 | tf_op jit(solution)/shard_map/ppermute | solution.py:14
  (103 other events, 1511.6 us)
where the time goes:
time: 430 us; the launch traced here: 423 us
  local copies, waits for them, and re-layouts  192 us (45%)
  blocking collectives  124 us (29%)
  other arithmetic  55.5 us (13%)
  starting transfers between devices  25.7 us (6%)
  matrix products  11.8 us (3%)
  waiting for transfers between devices  11 us (3%)
    all_gather x6, blocking collectives, level_conv(): face_frames = lax.all_gather(own_frame[None], 'patch', axis=0, tiled=True)  124 us
    slice x36, local copies, waits for them, and re-layouts, stencil(): padded[:, row_start:row_start + length, col_start:col_start + length]  46.7 us
    ppermute x24, starting transfers between devices, shifted(): lax.ppermute(array, axis, [(i, (i + by) % devices) for i in range(devices)])  25.7 us
    concatenate x6, local copies, waits for them, and re-layouts, stencil(): jnp.concatenate(columns, axis=0)  22 us
    rev x36, local copies, waits for them, and re-layouts, turn_once(): frames[..., 0, :, ::-1]  19.7 us
    rev x36, local copies, waits for them, and re-layouts, turn_once(): frames[..., 1, :, ::-1]  17.4 us
    select_n x18, other arithmetic, turned(): jnp.where((quarters == count)[:, None, None, None], current, result)  17.2 us
    reshape x16, local copies, waits for them, and re-layouts, stencil(): padded[:, row_start:row_start + length, col_start:col_start + length]  12.2 us
  transfers between devices with their start and end apart: 24, of which 10 were waited for; matrix products, arithmetic and copies ran while one was open for 3% of the time, Pallas kernels for 0%

commit v1 on v0

v1 whole, which is shorter than its diff:
```python
import functools
import math

import jax
import jax.numpy as jnp
from jax import lax
from jax.experimental import pallas as pl
from jax.experimental.pallas import tpu as pltpu
from jax.sharding import PartitionSpec as P

EPSILON = 1e-05
FLOOR_SQUARE = 0.5
MESH = pl.DeviceIdType.MESH
F32 = jnp.float32
BF16 = jnp.bfloat16

STEPS = ((-1, 0), (1, 0), (0, -1), (0, 1), (-1, -1), (-1, 1), (1, -1), (1, 1))
OPPOSITE = (1, 0, 3, 2, 7, 6, 5, 4)
READ_EDGE = (1, 0, 3, 2, 1, 1, 0, 0)
READ_LAST = (None, None, None, None, 1, 0, 1, 0)
SIDE_GAP = 8


def turned_source(edge, turns):
    flip = 0
    for _ in range(turns):
        if edge >= 2:
            flip ^= 1
        edge = (3, 2, 0, 1)[edge]
    return edge, flip


def corner_cell(direction, turns):
    edge, flip = turned_source(READ_EDGE[direction], turns)
    last = READ_LAST[direction] ^ flip
    return ((0, last), (1, last), (last, 0), (last, 1))[edge]


def pick(index, options):
    result = jnp.int32(options[0])
    for count in range(1, len(options)):
        result = jnp.where(index == count, jnp.int32(options[count]), result)
    return result


def grid_of(patches):
    rows = 1 << ((patches.bit_length() - 1) // 2)
    return rows, patches // rows


def pack_of(length, channels):
    return max(1, min(length // 16, 128 // channels))


def rim_shape(length, channels):
    count = pack_of(length, channels)
    return (length // count, channels * count)


def pack(edge):
    length, channels = edge.shape
    count = pack_of(length, channels)
    if count == 1:
        return edge
    step = length // count
    return jnp.concatenate([edge[i * step : (i + 1) * step] for i in range(count)], axis=1)


def unpack(rim, length, channels):
    count = pack_of(length, channels)
    if count == 1:
        return rim
    return jnp.concatenate([rim[:, i * channels : (i + 1) * channels] for i in range(count)], axis=0)


def activated(parts, films):
    channels = sum(part.shape[1] for part in parts)
    total = sum(jnp.sum(part * part, axis=1, keepdims=True) for part in parts)
    mean_square = total * (1.0 / channels)
    if channels >= 64:
        inverse = lax.rsqrt(mean_square + EPSILON)
    else:
        inverse = lax.rsqrt(jnp.maximum(mean_square, FLOOR_SQUARE))
    results = []
    for part, (scale, shift) in zip(parts, films):
        shaped = part * inverse * scale + shift
        results.append(shaped / (1.0 + jnp.exp(-shaped)))
    return results


def kernel(faces, patches, sizes, *refs):
    rows, cols = grid_of(patches)
    slots = 2 * (rows + cols)
    outers = 2 * cols + 2 * (rows - 2)
    shifts = 1 if faces == 2 else 2
    side, c1, c2, c3 = sizes
    mid, low = side // 2, side // 4
    (feat, f1, f2, f3, f4, f5, f6, w1, w2, w3, w4, w5, w6, link_patch, link_shift, link_turn, out) = refs[:17]
    scratch = refs[17:]
    p1, p2a, p2b, p3, keep1, keep2, keep3, up2, up1 = scratch[:9]
    rims, landed = scratch[9:15], scratch[15:21]
    near_send, far_send, recv = scratch[21:]

    face = lax.axis_index("face")
    me = lax.axis_index("patch")
    row, col = me // cols, me % cols
    top, bottom, left, right = row == 0, row == rows - 1, col == 0, col == cols - 1
    upright, across = jnp.logical_or(top, bottom), jnp.logical_or(left, right)
    outer = jnp.logical_or(upright, across)
    inside = []
    for dr, dc in STEPS:
        r, c = row + dr, col + dc
        inside.append(
            jnp.logical_and(
                jnp.logical_and(r >= 0, r < rows), jnp.logical_and(c >= 0, c < cols)
            )
        )

    def outer_patch(k):
        m = k - 2 * cols
        middle = (1 + m // 2) * cols + (m % 2) * (cols - 1)
        return jnp.where(k < cols, k, jnp.where(k < 2 * cols, (rows - 2) * cols + k, middle))

    def far_face(s):
        return lax.rem(face + (faces - 1 if s == 0 else 1), faces)

    barrier = pltpu.get_barrier_semaphore()
    for d, (dr, dc) in enumerate(STEPS):

        @pl.when(inside[d])
        def _(dr=dr, dc=dc):
            pl.semaphore_signal(
                barrier, inc=1, device_id=(face, me + dr * cols + dc), device_id_type=MESH
            )

    @pl.when(outer)
    def _():
        for s in range(shifts):

            def greet(k, carry, s=s):
                pl.semaphore_signal(
                    barrier, inc=1, device_id=(far_face(s), outer_patch(k)), device_id_type=MESH
                )
                return carry

            lax.fori_loop(0, outers, greet, 0)

    def meet():
        peers = sum(jnp.where(there, 1, 0) for there in inside)
        pl.semaphore_wait(barrier, peers + jnp.where(outer, outers * shifts, 0))

    where_from = []
    for d in range(8):
        q = link_patch[face, me, d]
        shift = link_shift[face, me, d]
        turn = link_turn[face, me, d]
        q_row, q_col = q // cols, q % cols
        if d < 4:
            edge = pick(turn, [turned_source(READ_EDGE[d], t)[0] for t in range(4)])
            flip = pick(turn, [turned_source(READ_EDGE[d], t)[1] for t in range(4)])
        else:
            last_row = pick(turn, [corner_cell(d, t)[0] for t in range(4)])
            last_col = pick(turn, [corner_cell(d, t)[1] for t in range(4)])
            on_row = q_row == last_row * (rows - 1)
            edge = jnp.where(on_row, last_row, 2 + last_col)
            flip = jnp.where(on_row, last_col, last_row)
            flip = jnp.where(shift == 0, jnp.int32(READ_LAST[d]), flip)
        slot = jnp.where(
            edge == 0,
            q_col,
            jnp.where(
                edge == 1,
                cols + q_col,
                jnp.where(edge == 2, 2 * cols + q_row, 2 * cols + rows + q_row),
            ),
        )
        group = jnp.where(shift < 0, slots, 0) if shifts == 2 else 0
        where_from.append((jnp.where(shift == 0, d, 8 + group + slot), flip))

    def sends(n, act):
        rim, land = rims[n], landed[n]
        for d, (dr, dc) in enumerate(STEPS):
            o = OPPOSITE[d]

            @pl.when(inside[d])
            def _(d=d, dr=dr, dc=dc, o=o):
                act(
                    pltpu.make_async_remote_copy(
                        src_ref=rim.at[READ_EDGE[o]],
                        dst_ref=land.at[o],
                        send_sem=near_send.at[d],
                        recv_sem=recv.at[n, o],
                        device_id=(face, me + dr * cols + dc),
                        device_id_type=MESH,
                    )
                )

        mine = (
            (upright, jnp.where(top, 0, 1), jnp.where(top, col, cols + col)),
            (across, jnp.where(left, 2, 3), jnp.where(left, 2 * cols + row, 2 * cols + rows + row)),
        )
        for way, (present, edge, slot) in enumerate(mine):

            @pl.when(present)
            def _(way=way, edge=edge, slot=slot):
                for s in range(shifts):

                    def one(k, carry, s=s):
                        place = 8 + s * slots + slot
                        act(
                            pltpu.make_async_remote_copy(
                                src_ref=rim.at[edge],
                                dst_ref=land.at[place],
                                send_sem=far_send.at[way, s, k],
                                recv_sem=recv.at[n, place],
                                device_id=(far_face(s), outer_patch(k)),
                                device_id_type=MESH,
                            )
                        )
                        return carry

                    lax.fori_loop(0, outers, one, 0)

    def arrive(n):
        rim, land = rims[n], landed[n]

        def wait(place):
            pltpu.make_async_remote_copy(
                src_ref=rim.at[0],
                dst_ref=land.at[place],
                send_sem=near_send.at[0],
                recv_sem=recv.at[n, place],
                device_id=(face, me),
                device_id_type=MESH,
            ).wait_recv()

        for d in range(8):

            @pl.when(inside[d])
            def _(d=d):
                wait(d)

        @pl.when(outer)
        def _():
            def one(k, carry):
                wait(8 + k)
                return carry

            lax.fori_loop(0, slots * shifts, one, 0)

    def exchange(n, length, fields):
        pitch = length + 2 * SIDE_GAP
        channels = sum(count for _, count in fields)
        starts = (
            pl.ds(pitch + SIDE_GAP, length),
            pl.ds(length * pitch + SIDE_GAP, length),
            pl.ds(pitch + SIDE_GAP, length, pitch),
            pl.ds(pitch + SIDE_GAP + length - 1, length, pitch),
        )
        for e, span in enumerate(starts):
            pieces = [ref[span, :][:, :count].astype(BF16) for ref, count in fields]
            edge = pieces[0] if len(pieces) == 1 else jnp.concatenate(pieces, axis=1)
            rims[n][e] = pack(edge)
        if n == 0:
            meet()
        sends(n, lambda copy: copy.start())
        arrive(n)
        line = lax.broadcasted_iota(jnp.int32, (length, length), 0)
        cell = lax.broadcasted_iota(jnp.int32, (length, length), 1)
        targets = (
            pl.ds(SIDE_GAP, length),
            pl.ds((length + 1) * pitch + SIDE_GAP, length),
            pl.ds(pitch + SIDE_GAP - 1, length, pitch),
            pl.ds(pitch + SIDE_GAP + length, length, pitch),
            pl.ds(SIDE_GAP - 1, 1),
            pl.ds(SIDE_GAP + length, 1),
            pl.ds((length + 1) * pitch + SIDE_GAP - 1, 1),
            pl.ds((length + 1) * pitch + SIDE_GAP + length, 1),
        )
        for d in range(8):
            place, flip = where_from[d]
            edge = unpack(landed[n][place], length, channels)
            if d < 4:
                order = jnp.where(cell == line + flip * (length - 1 - 2 * line), 1.0, 0.0)
                value = jnp.dot(order.astype(BF16), edge, preferred_element_type=F32)
            else:
                wide = edge.astype(F32)
                value = jnp.where(flip == 1, wide[length - 1 :], wide[:1])
            start = 0
            for ref, count in fields:
                piece = value[:, start : start + count]
                if count < 128:
                    piece = jnp.concatenate(
                        [piece, jnp.zeros((piece.shape[0], 128 - count), F32)], axis=1
                    )
                ref[targets[d], :] = piece
                start += count
        sends(n, lambda copy: copy.wait_send())

    def put(ref, base, length, count, values):
        pitch = length + 2 * SIDE_GAP
        for i in range(values.shape[0] // length):
            start = pl.multiple_of(base * pitch, 8) + (i + 1) * pitch + SIDE_GAP
            ref[pl.ds(start, length), :count] = values[i * length : (i + 1) * length]

    def conv(base, step, length, fields):
        pitch = length + 2 * SIDE_GAP
        total = None
        for ref, count, weight in fields:
            for u in range(3):
                for v in range(3):
                    lines = []
                    for i in range(step):
                        start = pl.multiple_of(base * pitch, 8) + (i + u) * pitch + SIDE_GAP - 1 + v
                        lines.append(ref[pl.ds(start, length), :][:, :count].astype(BF16))
                    block = lines[0] if step == 1 else jnp.concatenate(lines, axis=0)
                    term = lax.dot_general(
                        block,
                        weight[3 * u + v],
                        (((1,), (1,)), ((), ())),
                        preferred_element_type=F32,
                    )
                    total = term if total is None else total + term
        return total

    def film_of(ref, start, count):
        return (1.0 + ref[0:1, start : start + count], ref[1:2, start : start + count])

    def loop(count, body):
        def run(i, carry):
            body(i)
            return carry

        lax.fori_loop(0, count, run, 0)

    def coarse(ref, base, step, length, count):
        half = length // 2
        lines = []
        for i in range(step):
            start = pl.multiple_of(base * 2 * length, 8) + 2 * i * length
            quad = [
                ref[pl.ds(start + a * length + b, half, 2), :][:, :count]
                for a in range(2)
                for b in range(2)
            ]
            lines.append((quad[0] + quad[1] + (quad[2] + quad[3])) * 0.25)
        return lines[0] if step == 1 else jnp.concatenate(lines, axis=0)

    def spread(ref, base, step, length, values):
        for i in range(step):
            line = values[i * length : (i + 1) * length]
            start = pl.multiple_of(base * 4 * length, 8) + 4 * i * length
            for a in range(2):
                for b in range(2):
                    ref[pl.ds(start + 2 * a * length + b, length, 2), :] = line

    def lanes(values):
        count = values.shape[1]
        if count == 128:
            return values
        return jnp.concatenate([values, jnp.zeros((values.shape[0], 128 - count), F32)], axis=1)

    step = 8
    cells = step * side
    film1 = film_of(f1, 0, c1)

    def enter(i):
        start = pl.multiple_of(i * cells, cells)
        values = feat[:, pl.ds(start, cells)].astype(F32).T
        keep1[pl.ds(start, cells), :c1] = values
        put(p1, i * step, side, c1, activated([values], [film1])[0])

    loop(side // step, enter)
    exchange(0, side, [(p1, c1)])

    def first(i):
        start = pl.multiple_of(i * cells, cells)
        values = conv(i * step, step, side, [(p1, c1, w1)])
        keep1[pl.ds(start, cells), :c1] = keep1[pl.ds(start, cells), :c1] + values

    loop(side // step, first)

    step2 = 8
    cells2 = step2 * mid
    film2 = film_of(f2, 0, c1)

    def shrink(i):
        values = coarse(keep1, i * step2, step2, side, c1)
        put(p2a, i * step2, mid, c1, activated([values], [film2])[0])

    loop(mid // step2, shrink)
    exchange(1, mid, [(p2a, c1)])

    def second(i):
        start = pl.multiple_of(i * cells2, cells2)
        keep2[pl.ds(start, cells2), :c2] = conv(i * step2, step2, mid, [(p2a, c1, w2)])

    loop(mid // step2, second)

    put(p3, 0, low, c2, activated([coarse(keep2, 0, low, mid, c2)], [film_of(f3, 0, c2)])[0])
    exchange(2, low, [(p3, c2)])
    keep3[...] = conv(0, low, low, [(p3, c2, w3)])
    put(p3, 0, low, c3, activated([keep3[...]], [film_of(f4, 0, c3)])[0])
    exchange(3, low, [(p3, c3)])
    spread(up2, 0, low, low, keep3[...] + conv(0, low, low, [(p3, c3, w4)]))

    films5 = [film_of(f5, 0, c3), film_of(f5, c3, c2)]

    def join_middle(i):
        start = pl.multiple_of(i * cells2, cells2)
        skip = keep2[pl.ds(start, cells2), :c2].astype(BF16).astype(F32)
        one, two = activated([up2[pl.ds(start, cells2), :], skip], films5)
        put(p2a, i * step2, mid, c3, one)
        put(p2b, i * step2, mid, c2, two)

    loop(mid // step2, join_middle)
    exchange(4, mid, [(p2a, c3), (p2b, c2)])

    def fifth(i):
        values = conv(
            i * step2,
            step2,
            mid,
            [(p2a, c3, w5.at[:, :, :c3]), (p2b, c2, w5.at[:, :, c3:])],
        )
        spread(up1, i * step2, step2, mid, lanes(values))

    loop(mid // step2, fifth)

    film6 = [film_of(f6, 0, c2 + c1)]

    def join_fine(i):
        start = pl.multiple_of(i * cells, cells)
        skip = keep1[pl.ds(start, cells), :c1].astype(BF16).astype(F32)
        values = jnp.concatenate([up1[pl.ds(start, cells), :c2], skip], axis=1)
        put(p1, i * step, side, c2 + c1, activated([values], film6)[0])

    loop(side // step, join_fine)
    exchange(5, side, [(p1, c2 + c1)])

    def last(i):
        start = pl.multiple_of(i * cells, cells)
        skip = keep1[pl.ds(start, cells), :c1].astype(BF16).astype(F32)
        values = skip + conv(i * step, step, side, [(p1, c2 + c1, w6)])
        out[:, pl.ds(start, cells)] = values.T.astype(BF16)

    loop(side // step, last)


def body(faces, patches, features, f1, w1, f2, w2, f3, w3, f4, w4, f5, w5, f6, w6, *tables):
    c1, _, count = features.shape
    c2, c3 = w2.shape[0], w3.shape[0]
    side = math.isqrt(count)
    mid, low = side // 2, side // 4
    rows, cols = grid_of(patches)
    slots = 2 * (rows + cols)
    outers = 2 * cols + 2 * (rows - 2)
    shifts = 1 if faces == 2 else 2
    places = 8 + slots * shifts

    def taps(weight):
        return weight.reshape(weight.shape[0], 9, -1).transpose(1, 0, 2)

    def padded(length):
        return pltpu.VMEM(((length + 2) * (length + 2 * SIDE_GAP), 128), F32)

    shapes = [
        rim_shape(side, c1),
        rim_shape(mid, c1),
        rim_shape(low, c2),
        rim_shape(low, c3),
        rim_shape(mid, c3 + c2),
        rim_shape(side, c2 + c1),
    ]
    vmem = pl.BlockSpec(memory_space=pltpu.VMEM)
    smem = pl.BlockSpec(memory_space=pltpu.SMEM)
    result = pl.pallas_call(
        functools.partial(kernel, faces, patches, (side, c1, c2, c3)),
        out_shape=jax.ShapeDtypeStruct((c1, count), BF16),
        in_specs=[vmem] * 13 + [smem] * 3,
        out_specs=vmem,
        scratch_shapes=[
            padded(side),
            padded(mid),
            padded(mid),
            padded(low),
            pltpu.VMEM((count, 128), F32),
            pltpu.VMEM((count // 4, 128), F32),
            pltpu.VMEM((count // 16, 128), F32),
            pltpu.VMEM((count // 4, 128), F32),
            pltpu.VMEM((count, 128), F32),
        ]
        + [pltpu.VMEM((4,) + shape, BF16) for shape in shapes]
        + [pltpu.VMEM((places,) + shape, BF16) for shape in shapes]
        + [
            pltpu.SemaphoreType.DMA((8,)),
            pltpu.SemaphoreType.DMA((2, shifts, outers)),
            pltpu.SemaphoreType.DMA((6, places)),
        ],
        compiler_params=pltpu.CompilerParams(
            collective_id=0, has_side_effects=True, vmem_limit_bytes=56 * 1024 * 1024
        ),
    )(
        features[:, 0, :],
        f1, f2, f3, f4, f5, f6,
        taps(w1), taps(w2), taps(w3), taps(w4), taps(w5), taps(w6),
        *tables,
    )
    return result[:, None, :]


def solution(mesh):
    spec = P(None, "face", "patch")
    return jax.shard_map(
        functools.partial(body, mesh.shape["face"], mesh.shape["patch"]),
        mesh=mesh,
        in_specs=(spec,) + (P(),) * 15,
        out_specs=spec,
        check_vma=False,
    )
```

time: 430 us -> 74.4 us (0.17); the launches traced: 423 us -> 73.9 us
  local copies, waits for them, and re-layouts: 192 us -> 10.7 us
  blocking collectives: 124 us -> 0 us
  Pallas kernels: 0 us -> 63.1 us
  other arithmetic: 55.5 us -> 0 us
  starting transfers between devices: 25.7 us -> 0 us
  matrix products: 11.8 us -> 0 us
  waiting for transfers between devices: 11 us -> 0 us
    all_gather x6 -> x0, blocking collectives: 124 us -> none  [level_conv(): face_frames = lax.all_gather(own_frame[None], 'patch', axis=0, tiled=True)]
    pallas_call x0 -> x1, Pallas kernels: none -> 63.1 us  [body(): pl.pallas_call(functools.partial(kernel, faces, patches, (side, c1, c2, c...]
    slice x73 -> x0, local copies, waits for them, and re-layouts: 60.6 us -> none  [the longest x36 46.7 us: stencil(): padded[:, row_start:row_start + length, col_start:col_start + length]]
    rev x72 -> x0, local copies, waits for them, and re-layouts: 37.2 us -> none  [the longest x36 19.7 us: turn_once(): frames[..., 0, :, ::-1]]
    concatenate x9 -> x0, local copies, waits for them, and re-layouts: 27.6 us -> none  [the longest x6 22 us: stencil(): jnp.concatenate(columns, axis=0)]
    ppermute x24 -> x0, starting transfers between devices: 25.7 us -> none  [shifted(): lax.ppermute(array, axis, [(i, (i + by) % devices) for i in range(devices)])]
    select_n x32 -> x0, other arithmetic: 24.2 us -> none  [the longest x18 17.2 us: turned(): jnp.where((quarters == count)[:, None, None, None], current, result)]
    gather x18 -> x0, local copies, waits for them, and re-layouts: 18.6 us -> none  [the longest x12 12 us: pieces_for(): wanted = face_frames[link_patch[target_face, patch_id]]]
  transfers between devices with their start and end apart: 24 -> 0, of which waited for: 10 -> 0; matrix products, arithmetic and copies ran while one was open for 3% -> 0% of each run, Pallas kernels for 0% -> 0%
where the time goes in v1:
time: 74.4 us; the launch traced here: 73.9 us
  Pallas kernels  63.1 us (85%)
  local copies, waits for them, and re-layouts  10.7 us (14%)
    pallas_call x1, Pallas kernels, body(): pl.pallas_call(functools.partial(kernel, faces, patches, (side, c1, c2, c...  63.1 us
    reshape x8, local copies, waits for them, and re-layouts, taps(): return weight.reshape(weight.shape[0], 9, -1).transpose(1, 0, 2)  6.21 us
    unnamed x23, local copies, waits for them, and re-layouts  4.47 us

profile of v1, /device:TPU:0, one launch (start us, length us, event | category | flops | bytes accessed | tf_op | source)
XLA Modules:
  0.0 73.9 jit_solution(1686322677910458961)
XLA Ops:
  0.0 1.3 %reshape.22 = bf16[64,9,192]{2,1,0:T(8,128)(2,1)S(1)} reshape(bf16[64,1728]{1,0:T(8,128)(2,1)} %param.26) | data formatting | bytes 442368 | tf_op jit(solution)/shard_map/reshape | solution.py:462
  1.3 0.0 copy-start
  1.3 0.8 %copy.34 = bf16[64,9,192]{2,0,1:T(8,128)(2,1)} copy(bf16[64,9,192]{2,1,0:T(8,128)(2,1)S(1)} %reshape.22) | data formatting | bytes 442368 | tf_op jit(solution)/shard_map/reshape | solution.py:462
  2.1 0.1 copy-done
  2.3 0.2 copy.25
  2.5 0.9 %copy.26 = bf16[128,9,128]{2,0,1:T(8,128)(2,1)} copy(bf16[128,9,128]{0,2,1:T(8,128)(2,1)S(1)} %bitcast.16) | data formatting | bytes 589824 | tf_op jit(solution)/shard_map/reshape | solution.py:462
  3.4 0.0 copy-done.1
  3.4 0.9 %copy.24 = bf16[128,9,64]{2,0,1:T(8,128)(2,1)} copy(bf16[128,9,64]{0,2,1:T(8,128)(2,1)S(1)} %bitcast.27) | data formatting | bytes 294912 | tf_op jit(solution)/shard_map/reshape | solution.py:462
  4.3 0.1 copy.22
  4.4 0.8 %copy.23 = bf16[64,9,32]{2,0,1:T(8,128)(2,1)} copy(bf16[64,9,32]{0,2,1:T(8,128)(2,1)S(1)} %bitcast.22) | data formatting | bytes 73728 | tf_op jit(solution)/shard_map/reshape | solution.py:462
  5.2 0.0 copy-done.2
  5.3 0.1 reshape.23
  5.4 0.0 copy-start.4
  5.4 0.7 copy.35
  6.1 0.1 copy-done.4
  6.1 0.1 copy.20
  6.3 0.7 copy.21
  7.0 0.7 copy.29.refs_13_
  7.7 0.0 copy-done.6
  7.7 0.7 copy.30.refs_14_
  8.4 0.0 copy-done.7
  8.4 0.7 copy.31.refs_15_
  9.1 63.1 %shard_map.154 = bf16[32,4096]{1,0:T(8,128)(2,1)} custom-call(bf16[32,4096]{1,0:T(8,128)(2,1)} %bitcast.26, f32[2,32]{1,0:T(2,128)} %refs_1_.1, f32[2,32]{1,0:T(2,128)} %refs_2_.1, f32[2,64]{1,0:T(2,128)} %refs_3_.1, f32[2,128]{1,0:T(2,128)} %refs_4_.1, f32[2,192]{1,0:T(2,128)} %refs_5_.1, f32[2,96]{1,0:T(2,128)} %refs_6_.1, bf16[9,32,32]{2,1,0:T(8,128)(2,1)} %bitcast.25, ...), custom_call_target="tpu_custom_call" | custom-call | tf_op jit(solution)/shard_map/pallas_call | solution.py:477
  72.2 1.7 %copy.37 = bf16[32,1,4096]{2,0,1:T(8,128)(2,1)} copy(bf16[32,1,4096]{2,0,1:T(8,128)(2,1)} %bitcast.20) | data formatting | bytes 524288
  (8 shorter events, 0.0 us)
Async XLA Ops:
  1.3 1.0 %copy-start = (bf16[128,1152]{1,0:T(8,128)(2,1)S(1)}, bf16[128,1152]{1,0:T(8,128)(2,1)}, u32[]{:S(2)}) copy-start(bf16[128,1152]{1,0:T(8,128)(2,1)} %param.24) | copy-start | bytes 884740
  2.5 0.9 %copy-start.1 = (bf16[128,576]{0,1:T(8,128)(2,1)S(1)}, bf16[128,576]{0,1:T(8,128)(2,1)}, u32[]{:S(2)}) copy-start(bf16[128,576]{0,1:T(8,128)(2,1)} %param.22) | copy-start | bytes 442372
  3.4 0.9 %copy-start.3 = (bf16[64,288]{1,0:T(8,128)(2,1)S(1)}, bf16[64,288]{1,0:T(8,128)(2,1)}, u32[]{:S(2)}) copy-start(bf16[64,288]{1,0:T(8,128)(2,1)} %param.20) | copy-start | bytes 110596
  4.4 0.8 %copy-start.2 = (bf16[32,864]{1,0:T(8,128)(2,1)S(1)}, bf16[32,864]{1,0:T(8,128)(2,1)}, u32[]{:S(2)}) copy-start(bf16[32,864]{1,0:T(8,128)(2,1)} %param.28) | copy-start | bytes 165892
  5.4 0.7 %copy-start.4 = (bf16[32,288]{1,0:T(8,128)(2,1)S(1)}, bf16[32,288]{1,0:T(8,128)(2,1)}, u32[]{:S(2)}) copy-start(bf16[32,288]{1,0:T(8,128)(2,1)} %param.18) | copy-start | bytes 55300
  6.3 0.7 %copy-start.5 = (s32[2,16,8]{1,2,0:T(8,128)S(1)}, s32[2,16,8]{1,2,0:T(8,128)}, u32[]{:S(2)}) copy-start(s32[2,16,8]{1,2,0:T(8,128)} %param.29) | copy-start | bytes 3076
  7.0 0.7 copy-start.6
  7.7 0.7 copy-start.7

commit v2 on v1

--- a/solution.py
+++ b/solution.py
@@ -97,9 +97,10 @@
     mid, low = side // 2, side // 4
     (feat, f1, f2, f3, f4, f5, f6, w1, w2, w3, w4, w5, w6, link_patch, link_shift, link_turn, out) = refs[:17]
     scratch = refs[17:]
-    p1, p2a, p2b, p3, keep1, keep2, keep3, up2, up1 = scratch[:9]
-    rims, landed = scratch[9:15], scratch[15:21]
-    near_send, far_send, recv = scratch[21:]
+    p1, p2a, p2b, p3, keep1, keep2, keep3, up2, up1, mid5, ring, ring_b = scratch[:12]
+    t1, t2, t3, t4, t5a, t5b, t6 = scratch[12:19]
+    rims, landed = scratch[19:27], scratch[27:35]
+    near_send, far_send, recv = scratch[35:]
 
     face = lax.axis_index("face")
     me = lax.axis_index("patch")
@@ -151,9 +152,9 @@
 
     where_from = []
     for d in range(8):
-        q = link_patch[face, me, d]
-        shift = link_shift[face, me, d]
-        turn = link_turn[face, me, d]
+        q = link_patch[face, d, me]
+        shift = link_shift[face, d, me]
+        turn = link_turn[face, d, me]
         q_row, q_col = q // cols, q % cols
         if d < 4:
             edge = pick(turn, [turned_source(READ_EDGE[d], t)[0] for t in range(4)])
@@ -178,7 +179,7 @@
         where_from.append((jnp.where(shift == 0, d, 8 + group + slot), flip))
 
     def sends(n, act):
-        rim, land = rims[n], landed[n]
+        rim, land, lane = rims[n], landed[n], max(0, n - 5)
         for d, (dr, dc) in enumerate(STEPS):
             o = OPPOSITE[d]
 
@@ -188,7 +189,7 @@
                     pltpu.make_async_remote_copy(
                         src_ref=rim.at[READ_EDGE[o]],
                         dst_ref=land.at[o],
-                        send_sem=near_send.at[d],
+                        send_sem=near_send.at[lane, d],
                         recv_sem=recv.at[n, o],
                         device_id=(face, me + dr * cols + dc),
                         device_id_type=MESH,
@@ -211,7 +212,7 @@
                             pltpu.make_async_remote_copy(
                                 src_ref=rim.at[edge],
                                 dst_ref=land.at[place],
-                                send_sem=far_send.at[way, s, k],
+                                send_sem=far_send.at[lane, way, s, k],
                                 recv_sem=recv.at[n, place],
                                 device_id=(far_face(s), outer_patch(k)),
                                 device_id_type=MESH,
@@ -228,7 +229,7 @@
             pltpu.make_async_remote_copy(
                 src_ref=rim.at[0],
                 dst_ref=land.at[place],
-                send_sem=near_send.at[0],
+                send_sem=near_send.at[0, 0],
                 recv_sem=recv.at[n, place],
                 device_id=(face, me),
                 device_id_type=MESH,
@@ -248,53 +249,92 @@
 
             lax.fori_loop(0, slots * shifts, one, 0)
 
-    def exchange(n, length, fields):
-        pitch = length + 2 * SIDE_GAP
-        channels = sum(count for _, count in fields)
-        starts = (
-            pl.ds(pitch + SIDE_GAP, length),
-            pl.ds(length * pitch + SIDE_GAP, length),
-            pl.ds(pitch + SIDE_GAP, length, pitch),
-            pl.ds(pitch + SIDE_GAP + length - 1, length, pitch),
+    def launch(n, ref, base, pitch, length, count):
+        spans = (
+            pl.ds(base, length),
+            pl.ds(base + (length - 1) * pitch, length),
+            pl.ds(base, length, pitch),
+            pl.ds(base + length - 1, length, pitch),
         )
-        for e, span in enumerate(starts):
-            pieces = [ref[span, :][:, :count].astype(BF16) for ref, count in fields]
-            edge = pieces[0] if len(pieces) == 1 else jnp.concatenate(pieces, axis=1)
-            rims[n][e] = pack(edge)
+        for e, span in enumerate(spans):
+            rims[n][e] = pack(ref[span, :][:, :count].astype(BF16))
         if n == 0:
             meet()
         sends(n, lambda copy: copy.start())
-        arrive(n)
-        line = lax.broadcasted_iota(jnp.int32, (length, length), 0)
-        cell = lax.broadcasted_iota(jnp.int32, (length, length), 1)
-        targets = (
+
+    def launch_padded(n, ref, length, count):
+        pitch = length + 2 * SIDE_GAP
+        launch(n, ref, pitch + SIDE_GAP, pitch, length, count)
+
+    def gather(n, target, source_length, length, channels):
+        pitch = length + 2 * SIDE_GAP
+        ratio = length // source_length
+        line = lax.broadcasted_iota(jnp.int32, (length, source_length), 0) // ratio
+        cell = lax.broadcasted_iota(jnp.int32, (length, source_length), 1)
+        places = (
             pl.ds(SIDE_GAP, length),
-            pl.ds((length + 1) * pitch + SIDE_GAP, length),
-            pl.ds(pitch + SIDE_GAP - 1, length, pitch),
-            pl.ds(pitch + SIDE_GAP + length, length, pitch),
+            pl.ds(pitch + SIDE_GAP, length),
+            pl.ds(2 * pitch + SIDE_GAP, length),
+            pl.ds(3 * pitch + SIDE_GAP, length),
             pl.ds(SIDE_GAP - 1, 1),
             pl.ds(SIDE_GAP + length, 1),
-            pl.ds((length + 1) * pitch + SIDE_GAP - 1, 1),
-            pl.ds((length + 1) * pitch + SIDE_GAP + length, 1),
+            pl.ds(pitch + SIDE_GAP - 1, 1),
+            pl.ds(pitch + SIDE_GAP + length, 1),
         )
         for d in range(8):
             place, flip = where_from[d]
-            edge = unpack(landed[n][place], length, channels)
+            edge = unpack(landed[n][place], source_length, channels)
             if d < 4:
-                order = jnp.where(cell == line + flip * (length - 1 - 2 * line), 1.0, 0.0)
+                order = jnp.where(cell == line + flip * (source_length - 1 - 2 * line), 1.0, 0.0)
                 value = jnp.dot(order.astype(BF16), edge, preferred_element_type=F32)
             else:
                 wide = edge.astype(F32)
-                value = jnp.where(flip == 1, wide[length - 1 :], wide[:1])
-            start = 0
-            for ref, count in fields:
-                piece = value[:, start : start + count]
-                if count < 128:
-                    piece = jnp.concatenate(
-                        [piece, jnp.zeros((piece.shape[0], 128 - count), F32)], axis=1
+                value = jnp.where(flip == 1, wide[source_length - 1 :], wide[:1])
+            target[places[d], :channels] = value
+
+    def border(length, fields, target):
+        pitch = length + 2 * SIDE_GAP
+        for ref, count, _ in fields:
+            for side_base in (2 * pitch, 3 * pitch):
+                for end in (SIDE_GAP - 1, SIDE_GAP + length):
+                    ref[pl.ds(side_base + end, 1), :count] = jnp.zeros((1, count), F32)
+        spots = (
+            (0, pl.ds(0, length), (0, 1, 2)),
+            (1, pl.ds((length - 1) * length, length), (6, 7, 8)),
+            (2, pl.ds(0, length, length), (0, 3, 6)),
+            (3, pl.ds(length - 1, length, length), (2, 5, 8)),
+        )
+        for part, span, taps in spots:
+            total = None
+            for ref, count, weight in fields:
+                for move, tap in enumerate(taps):
+                    block = ref[pl.ds(part * pitch + SIDE_GAP - 1 + move, length), :count]
+                    term = lax.dot_general(
+                        block.astype(BF16),
+                        weight[tap],
+                        (((1,), (1,)), ((), ())),
+                        preferred_element_type=F32,
                     )
-                ref[targets[d], :] = piece
-                start += count
+                    total = term if total is None else total + term
+            target[span, :] = target[span, :] + lanes(total)
+
+    def clear(ref, length):
+        pitch = length + 2 * SIDE_GAP
+        for start in (0, (length + 1) * pitch):
+            ref[pl.ds(start, pitch), :] = jnp.zeros((pitch, 128), F32)
+        for start in (SIDE_GAP - 1, SIDE_GAP + length):
+            ref[pl.ds(pitch + start, length, pitch), :] = jnp.zeros((length, 128), F32)
+
+    def cut(weight, parts):
+        width = weight.shape[1] // 9
+        start = 0
+        for target in parts:
+            count = target.shape[2]
+            for k in range(9):
+                target[k] = weight[:, k * width + start : k * width + start + count]
+            start += count
+
+    def finish(n):
         sends(n, lambda copy: copy.wait_send())
 
     def put(ref, base, length, count, values):
@@ -371,14 +411,25 @@
         put(p1, i * step, side, c1, activated([values], [film1])[0])
 
     loop(side // step, enter)
-    exchange(0, side, [(p1, c1)])
+    launch_padded(0, p1, side, c1)
+    clear(p1, side)
+    cut(w1, [t1])
 
     def first(i):
         start = pl.multiple_of(i * cells, cells)
-        values = conv(i * step, step, side, [(p1, c1, w1)])
+        values = conv(i * step, step, side, [(p1, c1, t1)])
         keep1[pl.ds(start, cells), :c1] = keep1[pl.ds(start, cells), :c1] + values
 
     loop(side // step, first)
+    clear(p2a, mid)
+    clear(p2b, mid)
+    clear(p3, low)
+    cut(w2, [t2])
+    cut(w3, [t3])
+    arrive(0)
+    gather(0, ring, side, side, c1)
+    border(side, [(ring, c1, t1)], keep1)
+    finish(0)
 
     step2 = 8
     cells2 = step2 * mid
@@ -389,21 +440,41 @@
         put(p2a, i * step2, mid, c1, activated([values], [film2])[0])
 
     loop(mid // step2, shrink)
-    exchange(1, mid, [(p2a, c1)])
+    launch_padded(1, p2a, mid, c1)
+    launch(6, keep1, 0, side, side, c1)
 
     def second(i):
         start = pl.multiple_of(i * cells2, cells2)
-        keep2[pl.ds(start, cells2), :c2] = conv(i * step2, step2, mid, [(p2a, c1, w2)])
+        keep2[pl.ds(start, cells2), :c2] = conv(i * step2, step2, mid, [(p2a, c1, t2)])
 
     loop(mid // step2, second)
+    cut(w4, [t4])
+    arrive(1)
+    gather(1, ring, mid, mid, c1)
+    border(mid, [(ring, c1, t2)], keep2)
+    finish(1)
 
     put(p3, 0, low, c2, activated([coarse(keep2, 0, low, mid, c2)], [film_of(f3, 0, c2)])[0])
-    exchange(2, low, [(p3, c2)])
-    keep3[...] = conv(0, low, low, [(p3, c2, w3)])
+    launch_padded(2, p3, low, c2)
+    launch(7, keep2, 0, mid, mid, c2)
+    keep3[...] = conv(0, low, low, [(p3, c2, t3)])
+    cut(w5, [t5a, t5b])
+    arrive(2)
+    gather(2, ring, low, low, c2)
+    border(low, [(ring, c2, t3)], keep3)
+    finish(2)
+
     put(p3, 0, low, c3, activated([keep3[...]], [film_of(f4, 0, c3)])[0])
-    exchange(3, low, [(p3, c3)])
-    spread(up2, 0, low, low, keep3[...] + conv(0, low, low, [(p3, c3, w4)]))
-
+    launch_padded(3, p3, low, c3)
+    keep3[...] = keep3[...] + conv(0, low, low, [(p3, c3, t4)])
+    cut(w6, [t6])
+    arrive(3)
+    gather(3, ring, low, low, c3)
+    border(low, [(ring, c3, t4)], keep3)
+    finish(3)
+
+    launch(4, keep3, 0, low, low, c3)
+    spread(up2, 0, low, low, keep3[...])
     films5 = [film_of(f5, 0, c3), film_of(f5, c3, c2)]
 
     def join_middle(i):
@@ -414,19 +485,33 @@
         put(p2b, i * step2, mid, c2, two)
 
     loop(mid // step2, join_middle)
-    exchange(4, mid, [(p2a, c3), (p2b, c2)])
 
     def fifth(i):
-        values = conv(
-            i * step2,
-            step2,
-            mid,
-            [(p2a, c3, w5.at[:, :, :c3]), (p2b, c2, w5.at[:, :, c3:])],
+        start = pl.multiple_of(i * cells2, cells2)
+        mid5[pl.ds(start, cells2), :c2] = conv(
+            i * step2, step2, mid, [(p2a, c3, t5a), (p2b, c2, t5b)]
         )
-        spread(up1, i * step2, step2, mid, lanes(values))
 
     loop(mid // step2, fifth)
-
+    arrive(7)
+    arrive(4)
+    gather(7, ring_b, mid, mid, c2)
+    gather(4, ring, low, mid, c3)
+    extent = pl.ds(0, 4 * (mid + 2 * SIDE_GAP))
+    one, two = activated([ring[extent, :], ring_b[extent, :c2]], films5)
+    ring[extent, :] = one
+    ring_b[extent, :c2] = two
+    border(mid, [(ring, c3, t5a), (ring_b, c2, t5b)], mid5)
+    finish(7)
+    finish(4)
+
+    launch(5, mid5, 0, mid, mid, c2)
+
+    def widen(i):
+        start = pl.multiple_of(i * cells2, cells2)
+        spread(up1, i * step2, step2, mid, mid5[pl.ds(start, cells2), :])
+
+    loop(mid // step2, widen)
     film6 = [film_of(f6, 0, c2 + c1)]
 
     def join_fine(i):
@@ -436,15 +521,29 @@
         put(p1, i * step, side, c2 + c1, activated([values], film6)[0])
 
     loop(side // step, join_fine)
-    exchange(5, side, [(p1, c2 + c1)])
 
     def last(i):
         start = pl.multiple_of(i * cells, cells)
         skip = keep1[pl.ds(start, cells), :c1].astype(BF16).astype(F32)
-        values = skip + conv(i * step, step, side, [(p1, c2 + c1, w6)])
-        out[:, pl.ds(start, cells)] = values.T.astype(BF16)
+        keep1[pl.ds(start, cells), :c1] = skip + conv(i * step, step, side, [(p1, c2 + c1, t6)])
 
     loop(side // step, last)
+    arrive(6)
+    arrive(5)
+    gather(6, ring_b, side, side, c1)
+    gather(5, ring, mid, side, c2)
+    extent = pl.ds(0, 4 * (side + 2 * SIDE_GAP))
+    values = jnp.concatenate([ring[extent, :c2], ring_b[extent, :c1]], axis=1)
+    ring[extent, : c2 + c1] = activated([values], film6)[0]
+    border(side, [(ring, c2 + c1, t6)], keep1)
+
+    def leave(i):
+        start = pl.multiple_of(i * cells, cells)
+        out[:, pl.ds(start, cells)] = keep1[pl.ds(start, cells), :c1].T.astype(BF16)
+
+    loop(side // step, leave)
+    finish(6)
+    finish(5)
 
 
 def body(faces, patches, features, f1, w1, f2, w2, f3, w3, f4, w4, f5, w5, f6, w6, *tables):
@@ -458,9 +557,6 @@
     shifts = 1 if faces == 2 else 2
     places = 8 + slots * shifts
 
-    def taps(weight):
-        return weight.reshape(weight.shape[0], 9, -1).transpose(1, 0, 2)
-
     def padded(length):
         return pltpu.VMEM(((length + 2) * (length + 2 * SIDE_GAP), 128), F32)
 
@@ -469,8 +565,10 @@
         rim_shape(mid, c1),
         rim_shape(low, c2),
         rim_shape(low, c3),
-        rim_shape(mid, c3 + c2),
-        rim_shape(side, c2 + c1),
+        rim_shape(low, c3),
+        rim_shape(mid, c2),
+        rim_shape(side, c1),
+        rim_shape(mid, c2),
     ]
     vmem = pl.BlockSpec(memory_space=pltpu.VMEM)
     smem = pl.BlockSpec(memory_space=pltpu.SMEM)
@@ -489,13 +587,22 @@
             pltpu.VMEM((count // 16, 128), F32),
             pltpu.VMEM((count // 4, 128), F32),
             pltpu.VMEM((count, 128), F32),
+            pltpu.VMEM((count // 4, 128), F32),
+            pltpu.VMEM((4 * (side + 2 * SIDE_GAP), 128), F32),
+            pltpu.VMEM((4 * (side + 2 * SIDE_GAP), 128), F32),
+        ]
+        + [
+            pltpu.VMEM((9,) + shape, BF16)
+            for shape in (
+                (c1, c1), (c2, c1), (c3, c2), (c3, c3), (c2, c3), (c2, c2), (c1, c2 + c1)
+            )
         ]
         + [pltpu.VMEM((4,) + shape, BF16) for shape in shapes]
         + [pltpu.VMEM((places,) + shape, BF16) for shape in shapes]
         + [
-            pltpu.SemaphoreType.DMA((8,)),
-            pltpu.SemaphoreType.DMA((2, shifts, outers)),
-            pltpu.SemaphoreType.DMA((6, places)),
+            pltpu.SemaphoreType.DMA((3, 8)),
+            pltpu.SemaphoreType.DMA((3, 2, shifts, outers)),
+            pltpu.SemaphoreType.DMA((8, places)),
         ],
         compiler_params=pltpu.CompilerParams(
             collective_id=0, has_side_effects=True, vmem_limit_bytes=56 * 1024 * 1024
@@ -503,8 +610,8 @@
     )(
         features[:, 0, :],
         f1, f2, f3, f4, f5, f6,
-        taps(w1), taps(w2), taps(w3), taps(w4), taps(w5), taps(w6),
-        *tables,
+        w1, w2, w3, w4, w5, w6,
+        *(table.transpose(0, 2, 1) for table in tables),
     )
     return result[:, None, :]
 

time: 74.4 us -> 52.5 us (0.71)
  Pallas kernels: 63.1 us -> 48.9 us
  local copies, waits for them, and re-layouts: 10.7 us -> 3.38 us
    pallas_call x1, Pallas kernels: 63.1 us -> 48.9 us  [body(): pl.pallas_call(functools.partial(kernel, faces, patches, (side, c1, c2, c...]
    reshape x8 -> x0, local copies, waits for them, and re-layouts: 6.21 us -> none  [taps(): return weight.reshape(weight.shape[0], 9, -1).transpose(1, 0, 2)]
    unnamed x23 -> x2, local copies, waits for them, and re-layouts: 4.47 us -> 3.38 us
where the time goes in v2:
time: 52.5 us; the launch traced here: 52.3 us
  Pallas kernels  48.9 us (93%)
  local copies, waits for them, and re-layouts  3.38 us (6%)
    pallas_call x1, Pallas kernels, body(): pl.pallas_call(functools.partial(kernel, faces, patches, (side, c1, c2, c...  48.9 us
    unnamed x2, local copies, waits for them, and re-layouts  3.38 us

profile of v2, /device:TPU:0, one launch (start us, length us, event | category | flops | bytes accessed | tf_op | source)
XLA Modules:
  0.0 52.3 jit_solution(17910981017051201207)
XLA Ops:
  0.0 1.7 %copy.17.refs_9_ = bf16[128,576]{1,0:T(8,128)(2,1)} copy(bf16[128,576]{0,1:T(8,128)(2,1)} %param.22) | data formatting | bytes 294912 | tf_op args[6]
  1.7 48.9 %shard_map.154 = bf16[32,4096]{1,0:T(8,128)(2,1)} custom-call(bf16[32,4096]{1,0:T(8,128)(2,1)} %bitcast.6, f32[2,32]{1,0:T(2,128)} %refs_1_.1, f32[2,32]{1,0:T(2,128)} %refs_2_.1, f32[2,64]{1,0:T(2,128)} %refs_3_.1, f32[2,128]{1,0:T(2,128)} %refs_4_.1, f32[2,192]{1,0:T(2,128)} %refs_5_.1, f32[2,96]{1,0:T(2,128)} %refs_6_.1, bf16[32,288]{1,0:T(8,128)(2,1)} %refs_7_.1, ...), custom_call_target="tpu_custom_call" | custom-call | tf_op jit(solution)/shard_map/pallas_call | solution.py:575
  50.6 1.7 %copy.19 = bf16[32,1,4096]{2,0,1:T(8,128)(2,1)} copy(bf16[32,1,4096]{2,0,1:T(8,128)(2,1)} %bitcast.5) | data formatting | bytes 524288

commit v3 on v2

--- a/solution.py
+++ b/solution.py
@@ -117,10 +117,11 @@
             )
         )
 
-    def outer_patch(k):
-        m = k - 2 * cols
-        middle = (1 + m // 2) * cols + (m % 2) * (cols - 1)
-        return jnp.where(k < cols, k, jnp.where(k < 2 * cols, (rows - 2) * cols + k, middle))
+    outer_patches = [
+        p
+        for p in range(patches)
+        if p // cols in (0, rows - 1) or p % cols in (0, cols - 1)
+    ]
 
     def far_face(s):
         return lax.rem(face + (faces - 1 if s == 0 else 1), faces)
@@ -138,13 +139,10 @@
     def _():
         for s in range(shifts):
 
-            def greet(k, carry, s=s):
+            for p in outer_patches:
                 pl.semaphore_signal(
-                    barrier, inc=1, device_id=(far_face(s), outer_patch(k)), device_id_type=MESH
+                    barrier, inc=1, device_id=(far_face(s), p), device_id_type=MESH
                 )
-                return carry
-
-            lax.fori_loop(0, outers, greet, 0)
 
     def meet():
         peers = sum(jnp.where(there, 1, 0) for there in inside)
@@ -178,76 +176,80 @@
         group = jnp.where(shift < 0, slots, 0) if shifts == 2 else 0
         where_from.append((jnp.where(shift == 0, d, 8 + group + slot), flip))
 
-    def sends(n, act):
-        rim, land, lane = rims[n], landed[n], max(0, n - 5)
-        for d, (dr, dc) in enumerate(STEPS):
-            o = OPPOSITE[d]
-
-            @pl.when(inside[d])
-            def _(d=d, dr=dr, dc=dc, o=o):
-                act(
-                    pltpu.make_async_remote_copy(
-                        src_ref=rim.at[READ_EDGE[o]],
-                        dst_ref=land.at[o],
-                        send_sem=near_send.at[lane, d],
-                        recv_sem=recv.at[n, o],
-                        device_id=(face, me + dr * cols + dc),
-                        device_id_type=MESH,
-                    )
-                )
-
-        mine = (
-            (upright, jnp.where(top, 0, 1), jnp.where(top, col, cols + col)),
-            (across, jnp.where(left, 2, 3), jnp.where(left, 2 * cols + row, 2 * cols + rows + row)),
-        )
+    mine = (
+        (upright, jnp.where(top, 0, 1), jnp.where(top, col, cols + col)),
+        (across, jnp.where(left, 2, 3), jnp.where(left, 2 * cols + row, 2 * cols + rows + row)),
+    )
+
+    def near_copy(n, d):
+        dr, dc = STEPS[d]
+        o = OPPOSITE[d]
+        return pltpu.make_async_remote_copy(
+            src_ref=rims[n].at[READ_EDGE[o]],
+            dst_ref=landed[n].at[o],
+            send_sem=near_send.at[max(0, n - 5), d],
+            recv_sem=recv.at[n, o],
+            device_id=(face, me + dr * cols + dc),
+            device_id_type=MESH,
+        )
+
+    def start(n):
         for way, (present, edge, slot) in enumerate(mine):
 
             @pl.when(present)
             def _(way=way, edge=edge, slot=slot):
                 for s in range(shifts):
-
-                    def one(k, carry, s=s):
-                        place = 8 + s * slots + slot
-                        act(
-                            pltpu.make_async_remote_copy(
-                                src_ref=rim.at[edge],
-                                dst_ref=land.at[place],
-                                send_sem=far_send.at[lane, way, s, k],
-                                recv_sem=recv.at[n, place],
-                                device_id=(far_face(s), outer_patch(k)),
-                                device_id_type=MESH,
-                            )
-                        )
-                        return carry
-
-                    lax.fori_loop(0, outers, one, 0)
-
-    def arrive(n):
-        rim, land = rims[n], landed[n]
-
-        def wait(place):
-            pltpu.make_async_remote_copy(
-                src_ref=rim.at[0],
-                dst_ref=land.at[place],
-                send_sem=near_send.at[0, 0],
-                recv_sem=recv.at[n, place],
-                device_id=(face, me),
-                device_id_type=MESH,
-            ).wait_recv()
+                    for p in outer_patches:
+                        pltpu.make_async_remote_copy(
+                            src_ref=rims[n].at[edge],
+                            dst_ref=landed[n].at[8 + s * slots + slot],
+                            send_sem=far_send.at[max(0, n - 5), way],
+                            recv_sem=recv.at[n, 8],
+                            device_id=(far_face(s), p),
+                            device_id_type=MESH,
+                        ).start()
 
         for d in range(8):
 
             @pl.when(inside[d])
             def _(d=d):
-                wait(d)
+                near_copy(n, d).start()
+
+    def whole(n, count, sem, got):
+        span = landed[n].at[pl.ds(8, count)]
+        return pltpu.make_async_remote_copy(
+            src_ref=span,
+            dst_ref=span,
+            send_sem=sem,
+            recv_sem=got,
+            device_id=(face, me),
+            device_id_type=MESH,
+        )
+
+    def finish(n):
+        for way in range(2):
+
+            @pl.when(mine[way][0])
+            def _(way=way):
+                sem = far_send.at[max(0, n - 5), way]
+                whole(n, outers * shifts, sem, recv.at[n, 8]).wait_send()
+
+        for d in range(8):
+
+            @pl.when(inside[d])
+            def _(d=d):
+                near_copy(n, d).wait_send()
+
+    def arrive(n):
+        for d in range(8):
+
+            @pl.when(inside[d])
+            def _(d=d):
+                near_copy(n, OPPOSITE[d]).wait_recv()
 
         @pl.when(outer)
         def _():
-            def one(k, carry):
-                wait(8 + k)
-                return carry
-
-            lax.fori_loop(0, slots * shifts, one, 0)
+            whole(n, slots * shifts, far_send.at[0, 0], recv.at[n, 8]).wait_recv()
 
     def launch(n, ref, base, pitch, length, count):
         spans = (
@@ -260,7 +262,7 @@
             rims[n][e] = pack(ref[span, :][:, :count].astype(BF16))
         if n == 0:
             meet()
-        sends(n, lambda copy: copy.start())
+        start(n)
 
     def launch_padded(n, ref, length, count):
         pitch = length + 2 * SIDE_GAP
@@ -292,7 +294,7 @@
                 value = jnp.where(flip == 1, wide[source_length - 1 :], wide[:1])
             target[places[d], :channels] = value
 
-    def border(length, fields, target):
+    def border(length, fields, target, flat=0):
         pitch = length + 2 * SIDE_GAP
         for ref, count, _ in fields:
             for side_base in (2 * pitch, 3 * pitch):
@@ -312,7 +314,7 @@
                     term = lax.dot_general(
                         block.astype(BF16),
                         weight[tap],
-                        (((1,), (1,)), ((), ())),
+                        (((1,), (1 - flat,)), ((), ())),
                         preferred_element_type=F32,
                     )
                     total = term if total is None else total + term
@@ -334,16 +336,13 @@
                 target[k] = weight[:, k * width + start : k * width + start + count]
             start += count
 
-    def finish(n):
-        sends(n, lambda copy: copy.wait_send())
-
     def put(ref, base, length, count, values):
         pitch = length + 2 * SIDE_GAP
         for i in range(values.shape[0] // length):
             start = pl.multiple_of(base * pitch, 8) + (i + 1) * pitch + SIDE_GAP
             ref[pl.ds(start, length), :count] = values[i * length : (i + 1) * length]
 
-    def conv(base, step, length, fields):
+    def conv(base, step, length, fields, flat=0):
         pitch = length + 2 * SIDE_GAP
         total = None
         for ref, count, weight in fields:
@@ -357,7 +356,7 @@
                     term = lax.dot_general(
                         block,
                         weight[3 * u + v],
-                        (((1,), (1,)), ((), ())),
+                        (((1,), (1 - flat,)), ((), ())),
                         preferred_element_type=F32,
                     )
                     total = term if total is None else total + term
@@ -425,7 +424,8 @@
     clear(p2b, mid)
     clear(p3, low)
     cut(w2, [t2])
-    cut(w3, [t3])
+    for k in range(9):
+        t3[k] = w3[k * c2 : (k + 1) * c2, :]
     arrive(0)
     gather(0, ring, side, side, c1)
     border(side, [(ring, c1, t1)], keep1)
@@ -457,11 +457,11 @@
     put(p3, 0, low, c2, activated([coarse(keep2, 0, low, mid, c2)], [film_of(f3, 0, c2)])[0])
     launch_padded(2, p3, low, c2)
     launch(7, keep2, 0, mid, mid, c2)
-    keep3[...] = conv(0, low, low, [(p3, c2, t3)])
+    keep3[...] = conv(0, low, low, [(p3, c2, t3)], 1)
     cut(w5, [t5a, t5b])
     arrive(2)
     gather(2, ring, low, low, c2)
-    border(low, [(ring, c2, t3)], keep3)
+    border(low, [(ring, c2, t3)], keep3, 1)
     finish(2)
 
     put(p3, 0, low, c3, activated([keep3[...]], [film_of(f4, 0, c3)])[0])
@@ -594,15 +594,15 @@
         + [
             pltpu.VMEM((9,) + shape, BF16)
             for shape in (
-                (c1, c1), (c2, c1), (c3, c2), (c3, c3), (c2, c3), (c2, c2), (c1, c2 + c1)
+                (c1, c1), (c2, c1), (c2, c3), (c3, c3), (c2, c3), (c2, c2), (c1, c2 + c1)
             )
         ]
         + [pltpu.VMEM((4,) + shape, BF16) for shape in shapes]
         + [pltpu.VMEM((places,) + shape, BF16) for shape in shapes]
         + [
             pltpu.SemaphoreType.DMA((3, 8)),
-            pltpu.SemaphoreType.DMA((3, 2, shifts, outers)),
-            pltpu.SemaphoreType.DMA((8, places)),
+            pltpu.SemaphoreType.DMA((3, 2)),
+            pltpu.SemaphoreType.DMA((8, 9)),
         ],
         compiler_params=pltpu.CompilerParams(
             collective_id=0, has_side_effects=True, vmem_limit_bytes=56 * 1024 * 1024
@@ -610,7 +610,7 @@
     )(
         features[:, 0, :],
         f1, f2, f3, f4, f5, f6,
-        w1, w2, w3, w4, w5, w6,
+        w1, w2, w3.T, w4, w5, w6,
         *(table.transpose(0, 2, 1) for table in tables),
     )
     return result[:, None, :]

time: 52.5 us -> 46.4 us (0.88)
  Pallas kernels: 48.9 us -> 44.6 us
  local copies, waits for them, and re-layouts: 3.38 us -> 1.67 us
    pallas_call x1, Pallas kernels: 48.9 us -> 44.6 us  [body(): pl.pallas_call(functools.partial(kernel, faces, patches, (side, c1, c2, c...]
    unnamed x2 -> x1, local copies, waits for them, and re-layouts: 3.38 us -> 1.67 us
where the time goes in v3:
time: 46.4 us; the launch traced here: 46.3 us
  Pallas kernels  44.6 us (96%)
  local copies, waits for them, and re-layouts  1.67 us (4%)
    pallas_call x1, Pallas kernels, body(): pl.pallas_call(functools.partial(kernel, faces, patches, (side, c1, c2, c...  44.6 us
    unnamed x1, local copies, waits for them, and re-layouts  1.67 us

profile of v3, /device:TPU:0, one launch (start us, length us, event | category | flops | bytes accessed | tf_op | source)
XLA Modules:
  0.0 46.3 jit_solution(13419107838014677567)
XLA Ops:
  0.0 44.6 %shard_map.154 = bf16[32,4096]{1,0:T(8,128)(2,1)} custom-call(bf16[32,4096]{1,0:T(8,128)(2,1)} %bitcast.7, f32[2,32]{1,0:T(2,128)} %refs_1_.1, f32[2,32]{1,0:T(2,128)} %refs_2_.1, f32[2,64]{1,0:T(2,128)} %refs_3_.1, f32[2,128]{1,0:T(2,128)} %refs_4_.1, f32[2,192]{1,0:T(2,128)} %refs_5_.1, f32[2,96]{1,0:T(2,128)} %refs_6_.1, bf16[32,288]{1,0:T(8,128)(2,1)} %refs_7_.1, ...), custom_call_target="tpu_custom_call" | custom-call | tf_op jit(solution)/shard_map/pallas_call | solution.py:575
  44.6 1.7 %copy.18 = bf16[32,1,4096]{2,0,1:T(8,128)(2,1)} copy(bf16[32,1,4096]{2,0,1:T(8,128)(2,1)} %bitcast.6) | data formatting | bytes 524288
